TPU v7x, 32 devices: a whole 2x2x4 slice. The times are simulated.
32 devices in a mesh: groups: 2 (over y), blk: 4 (over z), split: 2 (over x), sub: 2 (over core).
Axes of the slice: x: 2, y: 2, z: 4, core: 2. Of those that a mesh axis runs over, the one named last changes fastest.
Arguments:
- attention_output_rows: bfloat16 [1024, 8192], P(('groups', 'blk'), 'split'), parts along dimension 0, may hold values from -6 to 6
- residual: bfloat16 [1024, 8192], P(('groups', 'split'), ('blk', 'sub')), parts along dimension 0, may hold values from -6 to 6
- output_projection_weight: bfloat16 [8192, 8192], P('split', ('blk', 'sub')), may hold values from -0.0625 to 0.0625
- down_adapter_bank: bfloat16 [4, 64, 8192], P('blk', None, 'split'), may hold values from -0.0625 to 0.0625
- up_adapter_bank: bfloat16 [4, 64, 8192], P('split', None, ('blk', 'sub')), may hold values from -0.75 to 0.75
- rollout_row_tenant: int32 [1024], P('groups'), parts along dimension 0, may hold values from 0 to 3, as said below
- tenant_bank_entry: int32 [4], replicated, may hold values from 0 to 3, each once
- tenant_live_rank: int32 [4], replicated, may hold values from 16 to 64, as said below
Outputs:
- layer_out: bfloat16 [1024, 8192], P(('groups', 'split'), ('blk', 'sub')), parts along dimension 0
There are 2 independent parts, one for each index of `groups`. A program takes and returns all parts, laid end to end along the dimension named above; an argument that names none is the same for every part. Nothing has to cross between parts.
Inputs may be any that keep to these rules, and one draw needn't show every extreme that they name: `rollout_row_tenant`: every tenant owns at least one row of every part. `tenant_live_rank`: some tenant has the full rank 64.
All inputs are finite; a program needn't handle non-finite values.
Results may differ from a plain program's by a relative error of at most 0.0038.
Values may be sent and summed in bfloat16 or wider, within the bound.
A program may use at most 64 MiB of HBM per device.

v0:
```python
import jax
import jax.numpy as jnp
from jax import lax
from jax.sharding import PartitionSpec as P


def shards(
    attention_output_rows,
    residual,
    output_projection_weight,
    down_adapter_bank,
    up_adapter_bank,
    rollout_row_tenant,
    tenant_bank_entry,
    tenant_live_rank,
):
    out_cols = output_projection_weight.shape[1]
    feat_width = attention_output_rows.shape[1]
    rank_mask_rows = down_adapter_bank.shape[1]
    gathered_down_maps = lax.all_gather(down_adapter_bank, "blk", axis=0, tiled=True)
    tenant_count = gathered_down_maps.shape[0]
    total_rows = rollout_row_tenant.shape[0]
    tenant_ids = jnp.arange(tenant_count, dtype=jnp.int32)
    tenant_hot = (rollout_row_tenant[:, None] == tenant_ids[None, :]).astype(jnp.int32)
    slot_all = jnp.sum(tenant_hot * tenant_bank_entry[None, :], axis=1)
    rank_all = jnp.sum(tenant_hot * tenant_live_rank[None, :], axis=1)
    down_cols = gathered_down_maps.reshape(tenant_count * rank_mask_rows, feat_width).T
    joined = jnp.concatenate([output_projection_weight, down_cols], axis=1)
    own_count = total_rows // lax.axis_size("split")
    own_start = lax.axis_index("split") * own_count
    own_slot = lax.dynamic_slice_in_dim(slot_all, own_start, own_count, 0)
    own_rank = lax.dynamic_slice_in_dim(rank_all, own_start, own_count, 0)
    own_hot = own_slot[:, None] == tenant_ids[None, :]
    full = jnp.dot(
        lax.all_gather(attention_output_rows, "blk", axis=0, tiled=True),
        joined,
        preferred_element_type=jnp.float32,
    )
    piece_hot = slot_all[:, None] == tenant_ids[None, :]
    values = full[:, out_cols:]
    shaped = values.reshape(values.shape[0], tenant_count, rank_mask_rows)
    products = jnp.concatenate(
        [
            full[:, :out_cols],
            jnp.sum(jnp.where(piece_hot[:, :, None], shaped, jnp.zeros((), jnp.float32)), axis=1),
        ],
        axis=1,
    )
    summed = lax.psum_scatter(products, "split", scatter_dimension=0, tiled=True)
    frozen_output_term = summed[:, :out_cols]
    low_rank = summed[:, out_cols:]
    gathered_up_maps = lax.all_gather(up_adapter_bank, "split", axis=0, tiled=True)
    kept_mask = jnp.arange(rank_mask_rows, dtype=jnp.int32)[None, :] < own_rank[:, None]
    scaling = rank_mask_rows / own_rank.astype(jnp.float32)
    low_scaled = jnp.where(
        kept_mask, low_rank * scaling[:, None], jnp.zeros((), jnp.float32)
    ).astype(jnp.bfloat16)
    rank_expanded_rows = jnp.where(
        own_hot[:, :, None], low_scaled[:, None, :], jnp.zeros((), jnp.bfloat16)
    ).reshape(own_count, tenant_count * rank_mask_rows)
    adapter_output_term = jnp.dot(
        rank_expanded_rows,
        gathered_up_maps.reshape(tenant_count * rank_mask_rows, out_cols),
        preferred_element_type=jnp.float32,
    )
    return (residual.astype(jnp.float32) + frozen_output_term + adapter_output_term).astype(
        jnp.bfloat16
    )


def solution(mesh):
    in_specs = (
        P(("groups", "blk"), "split"),
        P(("groups", "split"), ("blk", "sub")),
        P("split", ("blk", "sub")),
        P("blk", None, "split"),
        P("split", None, ("blk", "sub")),
        P("groups"),
        P(),
        P(),
    )
    out_specs = P(("groups", "split"), ("blk", "sub"))
    return jax.shard_map(shards, mesh=mesh, in_specs=in_specs, out_specs=out_specs, check_vma=False)
```

profile of v0, /device:TPU:0, one launch (start us, length us, event | category | flops | bytes accessed | tf_op | source)
XLA Modules:
  0.0 194.9 jit_solution(4081771632402627207)
XLA Ops:
  6.5 0.0 all-gather.3.cloned.1.call-start
  6.5 0.7 all-gather.3.cloned.1.call-update
  7.3 0.0 all-gather.5.cloned.1.call-start
  7.3 0.7 all-gather.5.cloned.1.call-update
  8.0 0.0 reduce-scatter.2.cloned.1.call-start
  8.1 0.8 select_reduce_fusion.1
  8.8 48.5 %all-gather.3.cloned.1.call-done = bf16[4,64,4096]{2,1,0:T(8,128)(2,1)} async-done(((bf16[1,64,4096]{2,1,0:T(8,128)(2,1)}), bf16[4,64,4096]{2,1,0:T(8,128)(2,1)}) %all-gather.3.cloned.1.call-update) | async-done | bytes 2097168 | tf_op jit(solution)/shard_map/all_gather | solution.py:20
  57.3 3.3 %copy.18 = bf16[256,4096]{0,1:T(8,128)(2,1)S(1)} copy(bf16[256,4096]{1,0:T(8,128)(2,1)} %bitcast.14) | data formatting | bytes 4194304 | tf_op jit(solution)/shard_map/reshape | solution.py:27
  60.6 77.9 %all-gather.5.cloned.1.call-done = bf16[512,4096]{1,0:T(8,128)(2,1)} async-done(((bf16[128,4096]{1,0:T(8,128)(2,1)}), bf16[512,4096]{1,0:T(8,128)(2,1)}) %all-gather.5.cloned.1.call-update) | async-done | bytes 4194320 | tf_op jit(solution)/shard_map/all_gather | solution.py:35
  138.5 9.7 %fusion.4 = f32[512,1280]{0,1:T(8,128)S(1)} fusion(bf16[512,4096]{1,0:T(8,128)(2,1)} %all-gather.5.cloned.1.call-done, bf16[4096,256]{1,0:T(8,128)(2,1)S(1)} %bitcast.15, bf16[4096,1024]{1,0:T(8,128)(2,1)} %param.10), kind=kOutput, calls=%fused_computation.4 | convolution fusion | flops 5389680640 | bytes 17301504 | tf_op jit(solution)/shard_map/dot_general | solution.py:34
  148.2 0.2 slice.16
  148.4 0.1 select_reduce_fusion
  148.5 0.0 copy-start
  148.5 1.6 pad_maximum_fusion
  150.0 0.0 copy-start.1
  150.0 0.0 reduce-scatter.2.cloned.1.call-update
  150.1 0.1 dynamic_slice.6
  150.1 0.0 copy-done
  150.1 0.2 copy.17
  150.4 0.1 convert_divide_fusion
  150.4 0.5 copy-done.1
  151.0 12.9 %all_gather.11 = bf16[4,64,1024]{2,1,0:T(8,128)(2,1)S(1)} all-gather(bf16[2,64,1024]{2,1,0:T(8,128)(2,1)S(1)} %copy-done.1), channel_id=1, replica_groups=mesh['groups'=2,'blk'=4,'split'=2,'sub'=2] {'split'}, dimensions={0}, use_global_device_ids=true | all-gather | bytes 786432 | tf_op jit(solution)/shard_map/all_gather | solution.py:52
  163.9 21.1 %reduce-scatter.2.cloned.1.call-done = f32[256,1088]{0,1:T(8,128)} async-done(((f32[512,1088]{0,1:T(8,128)}), f32[256,1088]{0,1:T(8,128)}) %reduce-scatter.2.cloned.1.call-update) | async-done | bytes 1114128 | tf_op jit(solution)/shard_map/reduce_scatter | solution.py:49
  185.0 0.9 fusion.12
  185.8 1.6 fusion.8
  187.4 1.0 copy.20
  (3 shorter events, 0.1 us)
Async XLA Ops:
  6.5 50.8 %all-gather.3.cloned.1.call-start = ((), (), s32[]{:S(2)}) async-start(), calls=%async_computation.1 | async-start | bytes 2621440 | tf_op jit(solution)/shard_map/all_gather | solution.py:20
  7.3 131.2 %all-gather.5.cloned.1.call-start = ((), (), s32[]{:S(2)}) async-start(), calls=%async_computation.2 | async-start | bytes 5242880 | tf_op jit(solution)/shard_map/all_gather | solution.py:35
  8.0 177.0 %reduce-scatter.2.cloned.1.call-start = ((), (), s32[]{:S(2)}) async-start(), calls=%async_computation.3 | async-start | bytes 3342336 | tf_op jit(solution)/shard_map/reduce_scatter | solution.py:49
  148.5 1.7 copy-start
  150.0 0.9 copy-start.1
Sparse Core Ops, SparseCore 0:
  8.9 48.3 all-gather.2
  58.9 79.5 all-gather.4
  150.2 34.7 reduce-scatter.1
where the time goes:
time: 195 us
  waiting for transfers between devices  149 us (76%)
  between operations  13.2 us (7%)
  blocking collectives  12.9 us (7%)
  matrix products  11.3 us (6%)
  local copies, waits for them, and re-layouts  5.31 us (3%)
  other arithmetic  3.35 us (2%)
    all_gather x1, waiting for transfers between devices, shards(): lax.all_gather(attention_output_rows, 'blk', axis=0, tiled=True)  77.9 us
    all_gather x1, waiting for transfers between devices, shards(): lax.all_gather(down_adapter_bank, 'blk', axis=0, tiled=True)  48.5 us
    reduce_scatter x1, waiting for transfers between devices, shards(): lax.psum_scatter(products, 'split', scatter_dimension=0, tiled=True)  21.1 us
    all_gather x1, blocking collectives, shards(): lax.all_gather(up_adapter_bank, 'split', axis=0, tiled=True)  12.9 us
    dot_general x1, matrix products, shards(): jnp.dot(lax.all_gather(attention_output_rows, 'blk', axis=0, tiled=True),...  9.71 us
  transfers between devices with their start and end apart: 3, of which 3 were waited for; matrix products, arithmetic and copies ran while one was open for 2% of the time, Pallas kernels for 0%

commit v1 on v0

--- a/solution.py
+++ b/solution.py
@@ -17,7 +17,14 @@
     out_cols = output_projection_weight.shape[1]
     feat_width = attention_output_rows.shape[1]
     rank_mask_rows = down_adapter_bank.shape[1]
-    gathered_down_maps = lax.all_gather(down_adapter_bank, "blk", axis=0, tiled=True)
+    size = lax.axis_size("blk")
+    right = [(i, (i + 1) % size) for i in range(size)]
+    parts = [down_adapter_bank]
+    for hop in range(1, size):
+        parts = [lax.ppermute(parts[0], "blk", right), *parts]
+    whole = jnp.concatenate(parts, axis=0)
+    places = (lax.axis_index("blk") + 1) * parts[-1].shape[0]
+    gathered_down_maps = jnp.roll(whole, places, axis=0)
     tenant_count = gathered_down_maps.shape[0]
     total_rows = rollout_row_tenant.shape[0]
     tenant_ids = jnp.arange(tenant_count, dtype=jnp.int32)

time: 195 us -> 172 us (0.88)
  waiting for transfers between devices: 149 us -> 108 us
  starting transfers between devices: 0.08 us -> 18.9 us
    ppermute x0 -> x3, waiting for transfers between devices: none -> 62.9 us  [shards(): parts = [lax.ppermute(parts[0], 'blk', right), *parts]]
    all_gather x1, waiting for transfers between devices: 77.9 us -> 22.3 us  [shards(): lax.all_gather(attention_output_rows, 'blk', axis=0, tiled=True)]
    all_gather x1 -> x0, waiting for transfers between devices: 48.5 us -> none  [shards(): lax.all_gather(down_adapter_bank, 'blk', axis=0, tiled=True)]
    ppermute x0 -> x3, starting transfers between devices: none -> 18.8 us  [shards(): parts = [lax.ppermute(parts[0], 'blk', right), *parts]]
    reshape x1 -> x0, local copies, waits for them, and re-layouts: 3.27 us -> none  [shards(): gathered_down_maps.reshape(tenant_count * rank_mask_rows, feat_width)]
    transpose x0 -> x1, local copies, waits for them, and re-layouts: none -> 2.47 us  [shards(): gathered_down_maps.reshape(tenant_count * rank_mask_rows, feat_width)]
  transfers between devices with their start and end apart: 3 -> 5, of which waited for: 3 -> 5; matrix products, arithmetic and copies ran while one was open for 2% -> 2% of each run, Pallas kernels for 0% -> 0%
where the time goes in v1:
time: 172 us
  waiting for transfers between devices  108 us (63%)
  starting transfers between devices  18.9 us (11%)
  between operations  13.6 us (8%)
  blocking collectives  12.1 us (7%)
  matrix products  11.2 us (7%)
  local copies, waits for them, and re-layouts  4.41 us (3%)
  other arithmetic  3.34 us (2%)
    ppermute x3, waiting for transfers between devices, shards(): parts = [lax.ppermute(parts[0], 'blk', right), *parts]  62.9 us
    all_gather x1, waiting for transfers between devices, shards(): lax.all_gather(attention_output_rows, 'blk', axis=0, tiled=True)  22.3 us
    reduce_scatter x1, waiting for transfers between devices, shards(): lax.psum_scatter(products, 'split', scatter_dimension=0, tiled=True)  22.2 us
    ppermute x3, starting transfers between devices, shards(): parts = [lax.ppermute(parts[0], 'blk', right), *parts]  18.8 us
    all_gather x1, blocking collectives, shards(): lax.all_gather(up_adapter_bank, 'split', axis=0, tiled=True)  12.1 us
    dot_general x1, matrix products, shards(): jnp.dot(lax.all_gather(attention_output_rows, 'blk', axis=0, tiled=True),...  9.64 us
  transfers between devices with their start and end apart: 5, of which 5 were waited for; matrix products, arithmetic and copies ran while one was open for 2% of the time, Pallas kernels for 0%

profile of v1, /device:TPU:0, one launch (start us, length us, event | category | flops | bytes accessed | tf_op | source)
XLA Modules:
  0.0 171.6 jit_solution(5337059086509351239)
XLA Ops:
  6.5 0.0 copy-start
  6.5 0.0 all-gather.2.cloned.1.call-start
  6.5 0.7 all-gather.2.cloned.1.call-update
  7.3 0.0 reduce-scatter.2.cloned.1.call-start
  7.3 3.1 %collective-permute-start = (bf16[1,64,4096]{2,1,0:T(8,128)(2,1)}, bf16[1,64,4096]{2,1,0:T(8,128)(2,1)S(1)}, u32[]{:S(2)}, u32[]{:S(2)}) collective-permute-start(bf16[1,64,4096]{2,1,0:T(8,128)(2,1)} %param.11), channel_id=1, source_target_pairs={{0,4},{4,8},{8,12},{12,0},{1,5},{5,9},{9,13},{13,1},{2,6},{6,10},{... | collective-permute-start | bytes 1572872 | tf_op jit(solution)/shard_map/ppermute | solution.py:24
  10.4 14.4 %collective-permute-done = bf16[1,64,4096]{2,1,0:T(8,128)(2,1)S(1)} collective-permute-done((bf16[1,64,4096]{2,1,0:T(8,128)(2,1)}, bf16[1,64,4096]{2,1,0:T(8,128)(2,1)S(1)}, u32[]{:S(2)}, u32[]{:S(2)}) %collective-permute-start) | collective-permute-done | bytes 524320 | tf_op jit(solution)/shard_map/ppermute | solution.py:24
  24.8 4.5 %collective-permute-start.1 = (bf16[1,64,4096]{2,1,0:T(8,128)(2,1)S(1)}, bf16[1,64,4096]{2,1,0:T(8,128)(2,1)S(1)}, u32[]{:S(2)}, u32[]{:S(2)}) collective-permute-start(bf16[1,64,4096]{2,1,0:T(8,128)(2,1)S(1)} %collective-permute-done), channel_id=1, source_target_pairs={{0,4},{4,8},{8,12},{12,0},{1,5},{5,9},{9,13},{13,1},{2,6},{6,10},{... | collective-permute-start | bytes 1572872 | tf_op jit(solution)/shard_map/ppermute | solution.py:24
  29.3 24.0 %collective-permute-done.1 = bf16[1,64,4096]{2,1,0:T(8,128)(2,1)S(1)} collective-permute-done((bf16[1,64,4096]{2,1,0:T(8,128)(2,1)S(1)}, bf16[1,64,4096]{2,1,0:T(8,128)(2,1)S(1)}, u32[]{:S(2)}, u32[]{:S(2)}) %collective-permute-start.1) | collective-permute-done | bytes 524320 | tf_op jit(solution)/shard_map/ppermute | solution.py:24
  53.3 11.2 %collective-permute-start.2 = (bf16[1,64,4096]{2,1,0:T(8,128)(2,1)S(1)}, bf16[1,64,4096]{2,1,0:T(8,128)(2,1)S(1)}, u32[]{:S(2)}, u32[]{:S(2)}) collective-permute-start(bf16[1,64,4096]{2,1,0:T(8,128)(2,1)S(1)} %collective-permute-done.1), channel_id=1, source_target_pairs={{0,4},{4,8},{8,12},{12,0},{1,5},{5,9},{9,13},{13,1},{2,6},{6,10},{... | collective-permute-start | bytes 1572872 | tf_op jit(solution)/shard_map/ppermute | solution.py:24
  64.6 0.8 select_reduce_fusion.1
  65.3 24.5 %collective-permute-done.2 = bf16[1,64,4096]{2,1,0:T(8,128)(2,1)S(1)} collective-permute-done((bf16[1,64,4096]{2,1,0:T(8,128)(2,1)S(1)}, bf16[1,64,4096]{2,1,0:T(8,128)(2,1)S(1)}, u32[]{:S(2)}, u32[]{:S(2)}) %collective-permute-start.2) | collective-permute-done | bytes 524320 | tf_op jit(solution)/shard_map/ppermute | solution.py:24
  90.0 0.0 copy-done
  90.2 0.1 constant_dynamic-slice_fusion
  90.4 2.5 %copy.21 = bf16[4096,256]{1,0:T(8,128)(2,1)} copy(bf16[4096,256]{0,1:T(8,128)(2,1)S(1)} %bitcast.14) | data formatting | bytes 4194304 | tf_op jit(solution)/shard_map/transpose | solution.py:34
  92.8 22.3 %all-gather.2.cloned.1.call-done = bf16[512,4096]{1,0:T(8,128)(2,1)} async-done(((bf16[128,4096]{1,0:T(8,128)(2,1)}), bf16[512,4096]{1,0:T(8,128)(2,1)}) %all-gather.2.cloned.1.call-update) | async-done | bytes 4194320 | tf_op jit(solution)/shard_map/all_gather | solution.py:42
  115.1 9.6 %fusion.4 = f32[512,1280]{0,1:T(8,128)S(1)} fusion(bf16[512,4096]{1,0:T(8,128)(2,1)} %all-gather.2.cloned.1.call-done, bf16[4096,256]{1,0:T(8,128)(2,1)} %copy.21, bf16[4096,1024]{1,0:T(8,128)(2,1)} %param.10), kind=kOutput, calls=%fused_computation.4 | convolution fusion | flops 5389680640 | bytes 17301504 | tf_op jit(solution)/shard_map/dot_general | solution.py:41
  124.7 0.2 slice.16
  124.9 0.0 copy-start.1
  125.0 0.0 copy-start.2
  125.0 0.1 select_reduce_fusion
  125.1 1.6 pad_maximum_fusion
  126.6 0.0 reduce-scatter.2.cloned.1.call-update
  126.6 0.1 dynamic_slice.11
  126.7 0.0 copy-done.1
  126.7 0.2 copy.20
  126.9 0.1 convert_divide_fusion
  127.0 0.0 copy-done.2
  127.0 12.1 %all_gather.7 = bf16[4,64,1024]{2,1,0:T(8,128)(2,1)S(1)} all-gather(bf16[2,64,1024]{2,1,0:T(8,128)(2,1)S(1)} %copy-done.2), channel_id=1, replica_groups=mesh['groups'=2,'blk'=4,'split'=2,'sub'=2] {'split'}, dimensions={0}, use_global_device_ids=true | all-gather | bytes 786432 | tf_op jit(solution)/shard_map/all_gather | solution.py:59
  139.1 22.2 %reduce-scatter.2.cloned.1.call-done = f32[256,1088]{0,1:T(8,128)} async-done(((f32[512,1088]{0,1:T(8,128)}), f32[256,1088]{0,1:T(8,128)}) %reduce-scatter.2.cloned.1.call-update) | async-done | bytes 1114128 | tf_op jit(solution)/shard_map/reduce_scatter | solution.py:56
  161.3 0.9 fusion.12
  162.2 1.6 fusion.8
  163.7 1.0 copy.23
  (11 shorter events, 0.3 us)
Async XLA Ops:
  6.5 83.4 %copy-start = (bf16[1,64,4096]{2,1,0:T(8,128)(2,1)S(1)}, bf16[1,64,4096]{2,1,0:T(8,128)(2,1)}, u32[]{:S(2)}) copy-start(bf16[1,64,4096]{2,1,0:T(8,128)(2,1)} %param.11) | copy-start | bytes 1572868
  6.5 108.6 %all-gather.2.cloned.1.call-start = ((), (), s32[]{:S(2)}) async-start(), calls=%async_computation.1 | async-start | bytes 5242880 | tf_op jit(solution)/shard_map/all_gather | solution.py:42
  7.3 154.1 %reduce-scatter.2.cloned.1.call-start = ((), (), s32[]{:S(2)}) async-start(), calls=%async_computation.2 | async-start | bytes 3342336 | tf_op jit(solution)/shard_map/reduce_scatter | solution.py:56
  7.3 17.5 %collective-permute-start = (bf16[1,64,4096]{2,1,0:T(8,128)(2,1)}, bf16[1,64,4096]{2,1,0:T(8,128)(2,1)S(1)}, u32[]{:S(2)}, u32[]{:S(2)}) collective-permute-start(bf16[1,64,4096]{2,1,0:T(8,128)(2,1)} %param.11), channel_id=1, source_target_pairs={{0,4},{4,8},{8,12},{12,0},{1,5},{5,9},{9,13},{13,1},{2,6},{6,10},{... | collective-permute-start | bytes 1572872 | tf_op jit(solution)/shard_map/ppermute | solution.py:24
  24.8 28.5 %collective-permute-start.1 = (bf16[1,64,4096]{2,1,0:T(8,128)(2,1)S(1)}, bf16[1,64,4096]{2,1,0:T(8,128)(2,1)S(1)}, u32[]{:S(2)}, u32[]{:S(2)}) collective-permute-start(bf16[1,64,4096]{2,1,0:T(8,128)(2,1)S(1)} %collective-permute-done), channel_id=1, source_target_pairs={{0,4},{4,8},{8,12},{12,0},{1,5},{5,9},{9,13},{13,1},{2,6},{6,10},{... | collective-permute-start | bytes 1572872 | tf_op jit(solution)/shard_map/ppermute | solution.py:24
  53.3 36.5 %collective-permute-start.2 = (bf16[1,64,4096]{2,1,0:T(8,128)(2,1)S(1)}, bf16[1,64,4096]{2,1,0:T(8,128)(2,1)S(1)}, u32[]{:S(2)}, u32[]{:S(2)}) collective-permute-start(bf16[1,64,4096]{2,1,0:T(8,128)(2,1)S(1)} %collective-permute-done.1), channel_id=1, source_target_pairs={{0,4},{4,8},{8,12},{12,0},{1,5},{5,9},{9,13},{13,1},{2,6},{6,10},{... | collective-permute-start | bytes 1572872 | tf_op jit(solution)/shard_map/ppermute | solution.py:24
  124.9 1.8 %copy-start.1 = (bf16[256,1024]{1,0:T(8,128)(2,1)S(1)}, bf16[256,1024]{1,0:T(8,128)(2,1)}, u32[]{:S(2)}) copy-start(bf16[256,1024]{1,0:T(8,128)(2,1)} %param.9) | copy-start | bytes 1572868
  125.0 2.0 %copy-start.2 = (bf16[2,64,1024]{2,1,0:T(8,128)(2,1)S(1)}, bf16[2,64,1024]{2,1,0:T(8,128)(2,1)}, u32[]{:S(2)}) copy-start(bf16[2,64,1024]{2,1,0:T(8,128)(2,1)} %param.12) | copy-start | bytes 786436
Sparse Core Ops, SparseCore 0:
  8.9 106.1 all-gather.1
  126.8 34.5 reduce-scatter.1
